TPU v7x, 128 devices: a whole 4x4x4 slice. The times are simulated.
128 devices in a mesh: row: 8 (over z, core), col: 16 (over x, y).
Axes of the slice: x: 4, y: 4, z: 4, core: 2. Of those that a mesh axis runs over, the one named last changes fastest.
Arguments:
- offsets: float32 [8, 16, 2, 256], P('row', 'col'), may hold values from 0 to 1
- point_order: int32 [8, 16, 256], P('row', 'col'), may hold values from 0 to 255, each once within a row
- nugget: float32 [8, 16, 256], P('row', 'col'), may hold values from 1 to 4
- interp: float32 [8, 16, 128, 128], P('row', 'col'), may hold values from -0.5 to 0.5
Outputs:
- root_work: float32 [16384, 16384], P('row', 'col')
Inputs may be any that keep to these rules, and one draw needn't show every extreme that they name: `point_order`: each row lists every point of its box once; its first 128 entries name the box's skeleton points.
All inputs are finite; a program needn't handle non-finite values.
Results may differ from a plain program's by a relative error of at most 0.0001.
Values sent between devices are 32-bit elements; how exact they have to be, the bound alone decides.
A program may use at most 128 MiB of HBM per device.

v0:
```python
import jax
import jax.numpy as jnp
from jax import lax
from jax.sharding import PartitionSpec as P

PW = 512


kernel_amp = 0.015625
kernel_len = 0.5
highest = lax.Precision.HIGHEST


def extended(block, sides, width):
    for axis, dim in sides:
        count = lax.axis_size(axis)
        forward = [(i, i + 1) for i in range(count - 1)]
        backward = [(target, source) for source, target in forward]
        low = lax.ppermute(
            lax.slice_in_dim(block, block.shape[dim] - width, None, axis=dim), axis, forward
        )
        high = lax.ppermute(lax.slice_in_dim(block, 0, width, axis=dim), axis, backward)
        block = jnp.concatenate([low, block, high], axis=dim)
    return block


def shifted(block, axis, distance):
    devices = range(lax.axis_size(axis))
    route = [(i - distance, i) for i in devices if i - distance in devices]
    return lax.ppermute(block, axis, route)


def spread_2(value, axis, source):
    kept = jnp.where(lax.axis_index(axis) == source, value, 0).astype(value.dtype)
    return lax.psum(kept, axis)


def offsets_all():
    return [(a, b) for a in (-1, 0, 1) for b in (-1, 0, 1)]


def pairs_all():
    return [
        (e, m)
        for e in offsets_all()
        for m in offsets_all()
        if abs(m[0] - e[0]) <= 1 and abs(m[1] - e[1]) <= 1
    ]


def block_of(a, b):
    return (a + 1) * 3 + (b + 1)


def vector(along, across):
    return (along, across)


def kernel(left, right):
    gap_row = left[0][:, None] - right[0][None, :]
    gap_col = left[1][:, None] - right[1][None, :]
    return kernel_amp * jnp.exp(-jnp.sqrt(gap_row * gap_row + gap_col * gap_col) / kernel_len)


def cross_pair(stored, target, columns):
    pair_index = {pair: n for n, pair in enumerate(pairs_all())}
    left_rows = []
    right_rows = []
    for e in offsets_all():
        if abs(target[0] - e[0]) <= 1 and abs(target[1] - e[1]) <= 1:
            left_rows.append(stored[pair_index[e, (0, 0)]][:, :columns])
            right_rows.append(stored[pair_index[e, target]][:, :columns])
    return (jnp.concatenate(left_rows, axis=0), jnp.concatenate(right_rows, axis=0))


def cross_sum(stored, target, columns):
    left_rows, right_rows = cross_pair(stored, target, columns)
    return jnp.einsum("rk,rl->kl", left_rows, right_rows, precision=highest)


def eliminate(stored, near_matrix, interp_box):
    box_points = near_matrix.shape[0]
    skel_count = interp_box.shape[0]
    fill_blocks = [cross_sum(stored, m, box_points) for m in offsets_all()]
    matrix = near_matrix - jnp.concatenate(fill_blocks, axis=1)
    reduced_rows = matrix[skel_count:] - jnp.einsum(
        "sr,sk->rk", interp_box, matrix[:skel_count], precision=highest
    )
    centre = reduced_rows[:, 4 * box_points : 5 * box_points]
    reduced = centre[:, skel_count:] - jnp.einsum(
        "rs,st->rt", centre[:, :skel_count], interp_box, precision=highest
    )
    diag_factor = jnp.linalg.cholesky(reduced)
    return jax.scipy.linalg.solve_triangular(diag_factor, reduced_rows, lower=True)


def spread(factor_new, move_first, move_second, p):
    box_points = factor_new.shape[1] // 9

    def take_block(m):
        k = block_of(m[0], m[1])
        return factor_new[:, k * box_points : (k + 1) * box_points]

    placed = {}
    section_one = {}
    for s in (1, -1):
        listing = [vector(u, v) for u in (0, s) for v in (-1, 0, 1)]
        arrived = move_first(jnp.stack([take_block(m) for m in listing]), s)
        source = vector(-s, 0)
        section_one[s] = (source, listing, arrived)
        for n, m in enumerate(listing):
            placed[source, (m[0] + source[0], m[1] + source[1])] = arrived[n]
    for t in (1, -1):
        payload = []
        labels = []
        for m in [vector(u, v) for u in (-1, 0, 1) for v in (0, t)]:
            payload.append(take_block(m))
            labels.append(((0, 0), m))
        for s in (1, -1):
            source, listing, arrived = section_one[s]
            for n, m in enumerate(listing):
                if m[1 - p] in (0, t):
                    payload.append(arrived[n])
                    labels.append((source, m))
        arrived = move_second(jnp.stack(payload), t)
        sender_at = vector(0, -t)
        for n, (anchor, m) in enumerate(labels):
            source = (anchor[0] + sender_at[0], anchor[1] + sender_at[1])
            placed[source, (m[0] + source[0], m[1] + source[1])] = arrived[n]
    for m in offsets_all():
        placed[(0, 0), m] = take_block(m)
    return jnp.stack([placed[pair] for pair in pairs_all()])


def on_device(offsets, point_order, nugget, interp):
    row_at = lax.axis_index("row")
    col_at = lax.axis_index("col")
    row_count = lax.axis_size("row")
    col_count = lax.axis_size("col")
    box_points = offsets.shape[3]
    skel_count = interp.shape[2]
    red_count = interp.shape[3]
    corner = jnp.stack([row_at, col_at]).astype(jnp.float32)[:, None]
    points = jnp.take(offsets[0, 0] + corner, point_order[0, 0], axis=1)
    weights = jnp.take(nugget[0, 0], point_order[0, 0])
    interp_box = interp[0, 0]
    neighbour_points = extended(points[None, None], (("row", 0), ("col", 1)), 1)
    present = []
    kernel_blocks = []
    for a, b in offsets_all():
        inside = (
            (row_at + a >= 0)
            & (row_at + a < row_count)
            & (col_at + b >= 0)
            & (col_at + b < col_count)
        )
        present.append(inside.astype(jnp.float32))
        kernel_block = kernel(points, neighbour_points[a + 1, b + 1]) * present[-1]
        if (a, b) == (0, 0):
            kernel_block = kernel_block + jnp.diag(weights)
        kernel_blocks.append(kernel_block)
    near_matrix = jnp.concatenate(kernel_blocks, axis=1)

    def move_first(x, amount):
        return shifted(x, "row", amount)

    def move_second(x, amount):
        return shifted(x, "col", amount)

    leading = 0
    colour = 2 * (row_at % 2) + col_at % 2
    stored = jnp.zeros((len(pairs_all()), red_count, box_points), jnp.float32)
    for k in range(4):
        factor_new = lax.cond(
            colour == k,
            lambda s: eliminate(s, near_matrix, interp_box),
            lambda s: jnp.zeros((red_count, 9 * box_points), jnp.float32),
            stored,
        )
        stored = stored + spread(factor_new, move_first, move_second, leading)
    row_width = skel_count // row_count
    col_width = skel_count // col_count
    box_total = row_count * col_count
    weights_skel = weights[:skel_count]
    row_ids = jnp.arange(skel_count, dtype=jnp.int32).reshape(row_count, row_width)
    col_ids = jnp.arange(skel_count, dtype=jnp.int32).reshape(col_count, col_width)
    diag_piece = jnp.where(
        row_ids[:, None, :, None] == col_ids[None, :, None, :],
        weights_skel.reshape(row_count, row_width)[:, None, :, None],
        0.0,
    )
    pieces = []
    for k, m in enumerate(offsets_all()):
        left_rows, right_rows = cross_pair(stored, m, skel_count)
        fill_part = jnp.einsum(
            "rak,rbl->abkl",
            left_rows.reshape(-1, row_count, row_width),
            right_rows.reshape(-1, col_count, col_width),
            precision=highest,
        )
        if m == (0, 0):
            delta_block = diag_piece - fill_part
        else:
            delta_block = -fill_part
        pieces.append(delta_block * present[k])
    outgoing = jnp.stack(pieces, axis=2).reshape(box_total * 9, row_width * col_width)
    arrived = lax.all_to_all(outgoing, ("row", "col"), split_axis=0, concat_axis=0, tiled=True)
    received = jnp.transpose(arrived.reshape(box_total, 9, row_width, col_width), (1, 2, 0, 3))
    box_ids = jnp.arange(box_total, dtype=jnp.int32)
    src_rows = (box_ids // col_count)[:, None]
    src_cols = (box_ids % col_count)[:, None]
    all_skeleton = lax.all_gather(points[:, :skel_count][None], ("row", "col"), axis=0, tiled=True)
    row_part = lax.dynamic_slice_in_dim(all_skeleton, row_at * row_width, row_width, 2)
    col_part = lax.dynamic_slice_in_dim(all_skeleton, col_at * col_width, col_width, 2)
    row_coords = jnp.transpose(row_part, (1, 2, 0)).reshape(2, row_width * box_total)
    col_coords = jnp.transpose(col_part, (1, 2, 0)).reshape(2, col_width * box_total)
    placed = jnp.zeros((row_width, box_total, col_width, box_total), jnp.float32)
    for n, (a, b) in enumerate(offsets_all()):
        target = (src_rows + a) * col_count + src_cols + b
        living = (
            (src_rows + a >= 0)
            & (src_rows + a < row_count)
            & (src_cols + b >= 0)
            & (src_cols + b < col_count)
        )
        hit = (target == box_ids[None, :]) & living
        placed = jnp.where(hit[None, :, None, :], received[n][:, :, :, None], placed)
    delta_tile = placed.reshape(row_width * box_total, col_width * box_total)
    root_matrix = kernel(row_coords, col_coords) + delta_tile
    rows_here = root_matrix.shape[0]
    cols_here = root_matrix.shape[1]
    global_rows = row_at * rows_here + jnp.arange(rows_here, dtype=jnp.int32)
    global_cols = col_at * cols_here + jnp.arange(cols_here, dtype=jnp.int32)
    columns_out = []
    for p in range(2):
        first_col = p * PW
        owner_col = first_col // cols_here
        local_col = first_col % cols_here
        owner_row = first_col // rows_here
        local_row = first_col % rows_here
        own_slab = root_matrix[:, local_col : local_col + PW]
        slab_rows = spread_2(own_slab, "col", owner_col)
        diag_block = spread_2(slab_rows[local_row : local_row + PW], "row", owner_row)
        diag_factor = jnp.linalg.cholesky(diag_block)
        solved = jax.scipy.linalg.solve_triangular(diag_factor, slab_rows.T, lower=True).T
        pasted = lax.dynamic_update_slice(solved, diag_factor, (first_col - row_at * rows_here, 0))
        inside = (global_rows >= first_col) & (global_rows < first_col + PW)
        panel_rows = jnp.where(
            (global_rows < first_col)[:, None], 0.0, jnp.where(inside[:, None], pasted, solved)
        )
        first_global = col_at * cols_here
        holder = first_global // rows_here
        offset_rows = first_global - holder * rows_here
        panel_cols = spread_2(
            lax.dynamic_slice_in_dim(panel_rows, offset_rows, cols_here, 0), "row", holder
        )
        root_matrix = root_matrix - jnp.einsum(
            "rk,ck->rc", panel_rows, panel_cols, precision=highest
        )
        columns_out.append((owner_col, local_col, panel_rows))
    for owner_col, local_col, panel_rows in columns_out:
        current = root_matrix[:, local_col : local_col + PW]
        root_matrix = lax.dynamic_update_slice(
            root_matrix, jnp.where(col_at == owner_col, panel_rows, current), (0, local_col)
        )
    top_rows = min(2 * PW, rows_here)
    top_block = root_matrix[:top_rows]
    zero_mask = (global_rows[:top_rows, None] < 2 * PW) & (global_cols[None, :] >= 2 * PW)
    return lax.dynamic_update_slice(root_matrix, jnp.where(zero_mask, 0.0, top_block), (0, 0))


def solution(mesh):
    in_specs = (
        P("row", "col", None, None),
        P("row", "col", None),
        P("row", "col", None),
        P("row", "col", None, None),
    )
    out_specs = P("row", "col")
    return jax.shard_map(
        on_device, mesh=mesh, in_specs=in_specs, out_specs=out_specs, check_vma=False
    )
```

profile of v0, /device:TPU:1, one launch (start us, length us, event | category | flops | bytes accessed | tf_op | source)
XLA Modules:
  0.0 1653.0 jit_solution(10580641799856505549)
XLA Ops:
  32.1 21.4 %conditional.4 = (f32[128,256]{1,0:T(8,128)}, f32[128,256]{1,0:T(8,128)}, f32[128,256]{1,0:T(8,128)}, f32[128,256]{1,0:T(8,128)}, f32[128,256]{1,0:T(8,128)}, /*...) conditional(s32[]{:T(128)} %convert_element_type.56, () %tuple.65, ...), branch_computations={%region_0.1_spmd, %region_1.6_spmd} | conditional | flops 2442133504 | bytes 22315710 | solution.py:174
  72.4 37.2 %collective-permute-start.4 = (f32[6,128,256]{2,1,0:T(8,128)S(1)}, f32[6,128,256]{2,1,0:T(8,128)S(1)}, u32[]{:S(2)}, u32[]{:S(2)}) collective-permute-start(f32[6,128,256]{2,1,0:T(8,128)S(1)} %get-tuple-element.992), channel_id=1, source_target_pairs={{0,16},{16,32},{32,48},{48,64},{64,80},{80,96},{96,112},{1,17},{17... | collective-permute-start | bytes 2359304 | tf_op jit(solution)/shard_map/ppermute | solution.py:30
  130.3 28.6 %collective-permute-done.6 = f32[14,128,256]{2,1,0:T(8,128)} collective-permute-done((f32[14,128,256]{2,1,0:T(8,128)}, f32[14,128,256]{2,1,0:T(8,128)}, u32[]{:S(2)}, u32[]{:S(2)}) %collective-permute-start.6) | collective-permute-done | bytes 1835040 | tf_op jit(solution)/shard_map/ppermute | solution.py:30
  219.9 57.6 %collective-permute-start.10 = (f32[14,128,256]{2,1,0:T(8,128)S(1)}, f32[14,128,256]{2,1,0:T(8,128)S(1)}, u32[]{:S(2)}, u32[]{:S(2)}) collective-permute-start(f32[14,128,256]{2,1,0:T(8,128)S(1)} %get-tuple-element.880), channel_id=1, source_target_pairs={{0,1},{1,2},{2,3},{3,4},{4,5},{5,6},{6,7},{7,8},{8,9},{9,10},{10,1... | collective-permute-start | bytes 5505032 | tf_op jit(solution)/shard_map/ppermute | solution.py:30
  284.6 23.6 %collective-permute-done.10 = f32[14,128,256]{2,1,0:T(8,128)S(1)} collective-permute-done((f32[14,128,256]{2,1,0:T(8,128)S(1)}, f32[14,128,256]{2,1,0:T(8,128)S(1)}, u32[]{:S(2)}, u32[]{:S(2)}) %collective-permute-start.10) | collective-permute-done | bytes 1835040 | tf_op jit(solution)/shard_map/ppermute | solution.py:30
  324.1 69.2 %conditional.6 = (f32[1,128,256]{2,1,0:T(8,128)}, f32[1,128,256]{2,1,0:T(8,128)}, f32[1,128,256]{2,1,0:T(8,128)}, f32[1,128,256]{2,1,0:T(8,128)}, f32[1,128,256]...) conditional(s32[]{:T(128)} %convert_element_type.58, () %tuple.69, ...), branch_computations={%region_6.9_spmd, %region_7.10_spmd} | conditional | flops 5867831296 | bytes 52954240 | solution.py:174
  361.7 13.2 cholesky.378
  378.5 11.3 custom-call.37
  425.1 13.5 collective-permute-done.13
  445.6 88.6 %all-gather.1 = f32[128,2,128]{2,1,0:T(2,128)S(1)} all-gather(f32[1,2,128]{2,1,0:T(2,128)S(1)} %copy.132), channel_id=2, replica_groups=mesh['row'=8,'col'=16] {'row','col'}, dimensions={0}, use_global_device_ids=true | all-gather | bytes 132096 | tf_op jit(solution)/shard_map/all_gather | solution.py:212
  607.0 51.4 %collective-permute-start.18 = (f32[14,128,256]{2,1,0:T(8,128)}, f32[14,128,256]{2,1,0:T(8,128)}, u32[]{:S(2)}, u32[]{:S(2)}) collective-permute-start(f32[14,128,256]{2,1,0:T(8,128)} %get-tuple-element.864), channel_id=1, source_target_pairs={{0,1},{1,2},{2,3},{3,4},{4,5},{5,6},{6,7},{7,8},{8,9},{9,10},{10,1... | collective-permute-start | bytes 5505032 | tf_op jit(solution)/shard_map/ppermute | solution.py:30
  670.9 17.9 %collective-permute-done.18 = f32[14,128,256]{2,1,0:T(8,128)} collective-permute-done((f32[14,128,256]{2,1,0:T(8,128)}, f32[14,128,256]{2,1,0:T(8,128)}, u32[]{:S(2)}, u32[]{:S(2)}) %collective-permute-start.18) | collective-permute-done | bytes 1835040 | tf_op jit(solution)/shard_map/ppermute | solution.py:30
  763.7 12.1 all-to-all-start
  776.1 18.5 %all-to-all-done = f32[128,9,128]{2,1,0:T(8,128)S(1)} async-done(((f32[128,9,128]{2,1,0:T(8,128)}), f32[128,9,128]{2,1,0:T(8,128)S(1)}, u32[]{:S(2)}, u32[]{:S(2)}) %all-to-all-start) | async-done | bytes 589856 | tf_op jit(solution)/shard_map/all_to_all | solution.py:207
  812.9 99.1 %all-reduce.10.cloned.1.call-done = f32[2048,512]{0,1:T(8,128)} async-done(((f32[2048,512]{0,1:T(8,128)}), f32[2048,512]{0,1:T(8,128)}) %all-reduce.10.cloned.1.call-update) | async-done | bytes 4194320 | tf_op jit(solution)/shard_map/psum | solution.py:35
  914.9 60.5 %all-reduce.12.cloned.1.call-done = f32[512,512]{0,1:T(8,128)} async-done(((f32[512,512]{0,1:T(8,128)}), f32[512,512]{0,1:T(8,128)}) %all-reduce.12.cloned.1.call-update) | async-done | bytes 1048592 | tf_op jit(solution)/shard_map/psum | solution.py:35
  977.4 11.7 cholesky.402
  999.6 11.7 cholesky.421
  1022.8 11.7 cholesky.442
  1045.2 12.1 cholesky.459
  1070.9 39.3 %custom-call.42 = f32[4,128,128]{1,2,0:T(8,128)S(1)} custom-call(f32[4,128,128]{2,1,0:T(8,128)S(1)} %get-tuple-element.489), custom_call_target="InvertDiagBlocksLowerTriangular" | custom-call | tf_op jit(solution)/shard_map/jit(_solve_triangular)/triangular_solve | solution.py:245
  1128.5 65.4 %all-reduce.14.cloned.1.call-done = f32[1024,512]{0,1:T(8,128)} async-done(((f32[1024,512]{0,1:T(8,128)}), f32[1024,512]{0,1:T(8,128)}) %all-reduce.14.cloned.1.call-update) | async-done | bytes 2097168 | tf_op jit(solution)/shard_map/psum | solution.py:35
  1193.8 17.4 %convolution_subtract_fusion.5 = f32[2048,1024]{0,1:T(8,128)S(1)} fusion(f32[2048,1024]{0,1:T(8,128)} %copy-done.2, f32[2048,512]{0,1:T(8,128)} %copy-done.9, f32[1024,512]{0,1:T(8,128)} %all-reduce.14.cloned.1.call-done), kind=kOutput, calls=%fused_computation.563 | convolution fusion | flops 12886999040 | bytes 23068672 | tf_op jit(solution)/shard_map/rk,ck->rc/dot_general | solution.py:257
  1217.0 104.4 %all-reduce.16.cloned.1.call-done = f32[2048,512]{0,1:T(8,128)} async-done(((f32[2048,512]{0,1:T(8,128)}), f32[2048,512]{0,1:T(8,128)}) %all-reduce.16.cloned.1.call-update) | async-done | bytes 4194320 | tf_op jit(solution)/shard_map/psum | solution.py:35
  1323.9 61.0 %all-reduce.18.cloned.1.call-done = f32[512,512]{0,1:T(8,128)} async-done(((f32[512,512]{0,1:T(8,128)}), f32[512,512]{0,1:T(8,128)}) %all-reduce.18.cloned.1.call-update) | async-done | bytes 1048592 | tf_op jit(solution)/shard_map/psum | solution.py:35
  1386.9 11.7 cholesky.474
  1409.1 11.7 cholesky.493
  1432.5 11.7 cholesky.514
  1454.9 11.9 cholesky.531
  1480.5 39.3 %custom-call.46 = f32[4,128,128]{1,2,0:T(8,128)S(1)} custom-call(f32[4,128,128]{2,1,0:T(8,128)S(1)} %get-tuple-element.490), custom_call_target="InvertDiagBlocksLowerTriangular" | custom-call | tf_op jit(solution)/shard_map/jit(_solve_triangular)/triangular_solve | solution.py:245
  1538.0 65.4 %all-reduce.20.cloned.1.call-done = f32[1024,512]{0,1:T(8,128)} async-done(((f32[1024,512]{0,1:T(8,128)}), f32[1024,512]{0,1:T(8,128)}) %all-reduce.20.cloned.1.call-update) | async-done | bytes 2097168 | tf_op jit(solution)/shard_map/psum | solution.py:35
  1603.4 18.3 %convolution_subtract_fusion.4 = f32[2048,1024]{0,1:T(8,128)} fusion(f32[2048,1024]{0,1:T(8,128)} %copy-done.3, f32[2048,512]{0,1:T(8,128)} %copy-done.8, f32[1024,512]{0,1:T(8,128)} %all-reduce.20.cloned.1.call-done), kind=kOutput, calls=%fused_computation.562 | convolution fusion | flops 12886999040 | bytes 23068672 | tf_op jit(solution)/shard_map/rk,ck->rc/dot_general | solution.py:257
  (801 shorter events, 603.8 us)
Async XLA Ops:
  11.7 7.4 collective-permute-start
  16.6 6.3 collective-permute-start.1
  23.0 4.9 collective-permute-start.2
  26.2 4.4 collective-permute-start.3
  60.8 49.7 %copy-start.29 = (f32[1,128,256]{2,1,0:T(8,128)S(1)}, f32[1,128,256]{2,1,0:T(8,128)}, u32[]{:S(2)}) copy-start(f32[1,128,256]{2,1,0:T(8,128)} %copy-done.28) | copy-start | bytes 393220
  72.4 46.1 %collective-permute-start.4 = (f32[6,128,256]{2,1,0:T(8,128)S(1)}, f32[6,128,256]{2,1,0:T(8,128)S(1)}, u32[]{:S(2)}, u32[]{:S(2)}) collective-permute-start(f32[6,128,256]{2,1,0:T(8,128)S(1)} %get-tuple-element.992), channel_id=1, source_target_pairs={{0,16},{16,32},{32,48},{48,64},{64,80},{80,96},{96,112},{1,17},{17... | collective-permute-start | bytes 2359304 | tf_op jit(solution)/shard_map/ppermute | solution.py:30
  111.5 13.3 collective-permute-start.5
  126.4 32.5 %collective-permute-start.6 = (f32[14,128,256]{2,1,0:T(8,128)}, f32[14,128,256]{2,1,0:T(8,128)}, u32[]{:S(2)}, u32[]{:S(2)}) collective-permute-start(f32[14,128,256]{2,1,0:T(8,128)} %get-tuple-element.888), channel_id=1, source_target_pairs={{0,1},{1,2},{2,3},{3,4},{4,5},{5,6},{6,7},{7,8},{8,9},{9,10},{10,1... | collective-permute-start | bytes 5505032 | tf_op jit(solution)/shard_map/ppermute | solution.py:30
  129.0 35.5 %collective-permute-start.7 = (f32[14,128,256]{2,1,0:T(8,128)}, f32[14,128,256]{2,1,0:T(8,128)}, u32[]{:S(2)}, u32[]{:S(2)}) collective-permute-start(f32[14,128,256]{2,1,0:T(8,128)} %get-tuple-element.887), channel_id=1, source_target_pairs={{1,0},{2,1},{3,2},{4,3},{5,4},{6,5},{7,6},{8,7},{9,8},{10,9},{11,1... | collective-permute-start | bytes 5505032 | tf_op jit(solution)/shard_map/ppermute | solution.py:30
  187.3 21.1 %copy-start.13 = (f32[49,128,256]{2,1,0:T(8,128)S(1)}, f32[49,128,256]{2,1,0:T(8,128)}, u32[]{:S(2)}) copy-start(f32[49,128,256]{2,1,0:T(8,128)} %copy-done.12) | copy-start | bytes 19267588
  195.5 19.0 %collective-permute-start.8 = (f32[6,128,256]{2,1,0:T(8,128)S(1)}, f32[6,128,256]{2,1,0:T(8,128)S(1)}, u32[]{:S(2)}, u32[]{:S(2)}) collective-permute-start(f32[6,128,256]{2,1,0:T(8,128)S(1)} %get-tuple-element.980), channel_id=1, source_target_pairs={{0,16},{16,32},{32,48},{48,64},{64,80},{80,96},{96,112},{1,17},{17... | collective-permute-start | bytes 2359304 | tf_op jit(solution)/shard_map/ppermute | solution.py:30
  206.5 13.3 collective-permute-start.9
  219.9 88.4 %collective-permute-start.10 = (f32[14,128,256]{2,1,0:T(8,128)S(1)}, f32[14,128,256]{2,1,0:T(8,128)S(1)}, u32[]{:S(2)}, u32[]{:S(2)}) collective-permute-start(f32[14,128,256]{2,1,0:T(8,128)S(1)} %get-tuple-element.880), channel_id=1, source_target_pairs={{0,1},{1,2},{2,3},{3,4},{4,5},{5,6},{6,7},{7,8},{8,9},{9,10},{10,1... | collective-permute-start | bytes 5505032 | tf_op jit(solution)/shard_map/ppermute | solution.py:30
  278.5 35.0 %collective-permute-start.11 = (f32[14,128,256]{2,1,0:T(8,128)S(1)}, f32[14,128,256]{2,1,0:T(8,128)S(1)}, u32[]{:S(2)}, u32[]{:S(2)}) collective-permute-start(f32[14,128,256]{2,1,0:T(8,128)S(1)} %get-tuple-element.879), channel_id=1, source_target_pairs={{1,0},{2,1},{3,2},{4,3},{5,4},{6,5},{7,6},{8,7},{9,8},{10,9},{11,1... | collective-permute-start | bytes 5505032 | tf_op jit(solution)/shard_map/ppermute | solution.py:30
  412.4 10.8 collective-permute-start.12
  415.3 28.2 %copy-start.81 = (s32[1,1,256]{2,1,0:T(1,128)S(1)}, s32[1,1,256]{2,1,0:T(1,128)}, u32[]{:S(2)}) copy-start(s32[1,1,256]{2,1,0:T(1,128)} %param.19) | copy-start | bytes 3076
  415.3 30.2 %copy-start.40 = (f32[2,256]{0,1:T(8,128)S(1)}, f32[2,256]{0,1:T(8,128)}, u32[]{:S(2)}) copy-start(f32[2,256]{0,1:T(8,128)} %copy-done.39) | copy-start | bytes 6148
  417.2 21.4 %collective-permute-start.13 = (f32[6,128,256]{2,1,0:T(8,128)S(1)}, f32[6,128,256]{2,1,0:T(8,128)S(1)}, u32[]{:S(2)}, u32[]{:S(2)}) collective-permute-start(f32[6,128,256]{2,1,0:T(8,128)S(1)} %constant_dynamic-update-slice_fusion.302), channel_id=1, source_target_pairs={{16,0},{32,16},{48,32},{64,48},{80,64},{96,80},{112,96},{17,1},{33... | collective-permute-start | bytes 2359304 | tf_op jit(solution)/shard_map/ppermute | solution.py:30
  440.3 98.2 %collective-permute-start.14 = (f32[14,128,256]{2,1,0:T(8,128)}, f32[14,128,256]{2,1,0:T(8,128)}, u32[]{:S(2)}, u32[]{:S(2)}) collective-permute-start(f32[14,128,256]{2,1,0:T(8,128)} %get-tuple-element.872), channel_id=1, source_target_pairs={{0,1},{1,2},{2,3},{3,4},{4,5},{5,6},{6,7},{7,8},{8,9},{9,10},{10,1... | collective-permute-start | bytes 5505032 | tf_op jit(solution)/shard_map/ppermute | solution.py:30
  444.2 96.6 %collective-permute-start.15 = (f32[14,128,256]{2,1,0:T(8,128)}, f32[14,128,256]{2,1,0:T(8,128)}, u32[]{:S(2)}, u32[]{:S(2)}) collective-permute-start(f32[14,128,256]{2,1,0:T(8,128)} %get-tuple-element.871), channel_id=1, source_target_pairs={{1,0},{2,1},{3,2},{4,3},{5,4},{6,5},{7,6},{8,7},{9,8},{10,9},{11,1... | collective-permute-start | bytes 5505032 | tf_op jit(solution)/shard_map/ppermute | solution.py:30
  589.6 10.8 collective-permute-start.16
  592.2 13.3 collective-permute-start.17
  607.0 81.8 %collective-permute-start.18 = (f32[14,128,256]{2,1,0:T(8,128)}, f32[14,128,256]{2,1,0:T(8,128)}, u32[]{:S(2)}, u32[]{:S(2)}) collective-permute-start(f32[14,128,256]{2,1,0:T(8,128)} %get-tuple-element.864), channel_id=1, source_target_pairs={{0,1},{1,2},{2,3},{3,4},{4,5},{5,6},{6,7},{7,8},{8,9},{9,10},{10,1... | collective-permute-start | bytes 5505032 | tf_op jit(solution)/shard_map/ppermute | solution.py:30
  662.1 35.4 %collective-permute-start.19 = (f32[14,128,256]{2,1,0:T(8,128)S(1)}, f32[14,128,256]{2,1,0:T(8,128)S(1)}, u32[]{:S(2)}, u32[]{:S(2)}) collective-permute-start(f32[14,128,256]{2,1,0:T(8,128)S(1)} %get-tuple-element.863), channel_id=1, source_target_pairs={{1,0},{2,1},{3,2},{4,3},{5,4},{6,5},{7,6},{8,7},{9,8},{10,9},{11,1... | collective-permute-start | bytes 5505032 | tf_op jit(solution)/shard_map/ppermute | solution.py:30
  763.7 30.9 %all-to-all-start = ((f32[128,9,128]{2,1,0:T(8,128)}), f32[128,9,128]{2,1,0:T(8,128)S(1)}, u32[]{:S(2)}, u32[]{:S(2)}) async-start(f32[128,9,128]{2,1,0:T(8,128)} %copy.165), calls=%async_computation | async-start | bytes 2097152 | tf_op jit(solution)/shard_map/all_to_all | solution.py:207
  775.8 19.4 %copy-start.73 = (pred[128,128]{0,1:T(8,128)(4,1)S(1)}, pred[128,128]{0,1:T(8,128)(4,1)}, u32[]{:S(2)}) copy-start(pred[128,128]{0,1:T(8,128)(4,1)} %fusion.311) | copy-start | bytes 49156
  775.9 136.1 %all-reduce.10.cloned.1.call-start = ((), (), s32[]{:S(2)}) async-start(), calls=%async_computation.1 | async-start | bytes 8388608 | tf_op jit(solution)/shard_map/psum | solution.py:35
  812.8 162.6 %all-reduce.12.cloned.1.call-start = ((), (), s32[]{:S(2)}) async-start(), calls=%async_computation.2 | async-start | bytes 2097152 | tf_op jit(solution)/shard_map/psum | solution.py:35
  914.4 279.5 %all-reduce.14.cloned.1.call-start = ((), (), s32[]{:S(2)}) async-start(), calls=%async_computation.3 | async-start | bytes 4194304 | tf_op jit(solution)/shard_map/psum | solution.py:35
  1128.4 193.0 %all-reduce.16.cloned.1.call-start = ((), (), s32[]{:S(2)}) async-start(), calls=%async_computation.4 | async-start | bytes 8388608 | tf_op jit(solution)/shard_map/psum | solution.py:35
  1217.0 168.0 %all-reduce.18.cloned.1.call-start = ((), (), s32[]{:S(2)}) async-start(), calls=%async_computation.5 | async-start | bytes 2097152 | tf_op jit(solution)/shard_map/psum | solution.py:35
  1323.8 279.5 %all-reduce.20.cloned.1.call-start = ((), (), s32[]{:S(2)}) async-start(), calls=%async_computation.6 | async-start | bytes 4194304 | tf_op jit(solution)/shard_map/psum | solution.py:35
  (77 other events, 483.2 us)
Sparse Core Ops, SparseCore 0:
  813.0 98.9 all-reduce.9
  914.5 60.9 all-reduce.11
  1128.6 65.2 all-reduce.13
  1217.1 104.3 all-reduce.15
  1324.0 60.9 all-reduce.17
  1538.1 65.2 all-reduce.19
where the time goes:
time: 1660 us; the launch traced here: 1650 us
  waiting for transfers between devices  610 us (37%)
  other arithmetic  345 us (21%)
  local copies, waits for them, and re-layouts  267 us (16%)
  starting transfers between devices  203 us (12%)
  matrix products  92.8 us (6%)
  blocking collectives  88.6 us (5%)
  loops' own time  24.5 us (1%)
  between operations  22 us (1%)
    psum x6, waiting for transfers between devices, spread_2(): return lax.psum(kept, axis)  456 us
    ppermute x16, starting transfers between devices, shifted(): return lax.ppermute(block, axis, route)  179 us
    another operation x30, other arithmetic, on_device(): diag_factor = jnp.linalg.cholesky(diag_block)  159 us
    unnamed x365, local copies, waits for them, and re-layouts  152 us
    ppermute x16, waiting for transfers between devices, shifted(): return lax.ppermute(block, axis, route)  129 us
    all_gather x1, blocking collectives, on_device(): lax.all_gather(points[:, :skel_count][None], ('row', 'col'), axis=0, tile...  88.6 us
    another operation x7, other arithmetic, on_device(): jax.scipy.linalg.solve_triangular(diag_factor, slab_rows.T, lower=True)  81 us
    dot_general x2, matrix products, on_device(): jnp.einsum('rk,ck->rc', panel_rows, panel_cols, precision=highest)  35.6 us
  transfers between devices with their start and end apart: 27, of which 23 were waited for; matrix products, arithmetic and copies ran while one was open for 3% of the time, Pallas kernels for 0%

commit v1 on v0

--- a/solution.py
+++ b/solution.py
@@ -1,9 +1,12 @@
 import jax
 import jax.numpy as jnp
 from jax import lax
+from jax.experimental import pallas as pl
+from jax.experimental.pallas import tpu as pltpu
 from jax.sharding import PartitionSpec as P
 
 PW = 512
+SB = 1024
 
 
 kernel_amp = 0.015625
@@ -28,11 +31,6 @@
     devices = range(lax.axis_size(axis))
     route = [(i - distance, i) for i in devices if i - distance in devices]
     return lax.ppermute(block, axis, route)
-
-
-def spread_2(value, axis, source):
-    kept = jnp.where(lax.axis_index(axis) == source, value, 0).astype(value.dtype)
-    return lax.psum(kept, axis)
 
 
 def offsets_all():
@@ -132,6 +130,239 @@
     return jnp.stack([placed[pair] for pair in pairs_all()])
 
 
+def factor128(a):
+    n = a.shape[0]
+    G = n // 8
+    rows = [a[8*g:8*g+8] for g in range(G)]
+    lane = lax.broadcasted_iota(jnp.int32, (8, n), 1)
+    sub = lax.broadcasted_iota(jnp.int32, (8, n), 0)
+    w = [(lane == sub + 8*g).astype(jnp.float32) for g in range(G)]
+    def srow(v, t):
+        return jnp.broadcast_to(v[t:t+1], (8, n))
+    def lcol(v, t):
+        return jnp.broadcast_to(v[:, t:t+1], (8, n))
+    us, ws = [], []
+    for p in range(G):
+        q, qw = rows[p], w[p]
+        cols = [lcol(q, 8*p+t) for t in range(8)]
+        u, uw, dv = q, qw, None
+        for t in range(8):
+            pr, pw = srow(q, t), srow(qw, t)
+            d = srow(cols[t], t)
+            here = sub == t
+            u = pr if t == 0 else jnp.where(here, pr, u)
+            uw = pw if t == 0 else jnp.where(here, pw, uw)
+            dv = d if t == 0 else jnp.where(here, d, dv)
+            m = jnp.where(here, 0.0, cols[t]) * (1.0 / d)
+            q = q - m * pr
+            qw = qw - m * pw
+            for v in range(t + 1, 8):
+                cols[v] = cols[v] - m * srow(cols[v], t)
+        r = lax.rsqrt(dv)
+        us.append(jnp.where(lane >= sub + 8*p, u * r, 0.0))
+        ws.append(uw * r)
+        inv = 1.0 / dv
+        z, zw = q * inv, qw * inv
+        zs = [srow(z, t) for t in range(8)]
+        zws = [srow(zw, t) for t in range(8)]
+        for g in range(p + 1, G):
+            cg = [lcol(rows[g], 8*p+t) for t in range(8)]
+            x = [cg[t] * zs[t] for t in range(8)]
+            y = [cg[t] * zws[t] for t in range(8)]
+            rows[g] = rows[g] - (((x[0]+x[1])+(x[2]+x[3]))+((x[4]+x[5])+(x[6]+x[7])))
+            w[g] = w[g] - (((y[0]+y[1])+(y[2]+y[3]))+((y[4]+y[5])+(y[6]+y[7])))
+    return jnp.concatenate(us, 0), jnp.concatenate(ws, 0)
+
+
+def split(x):
+    hi = x.astype(jnp.bfloat16)
+    return hi, (x - hi.astype(jnp.float32)).astype(jnp.bfloat16)
+
+
+def dot3(a, b, dims):
+    def one(x, y):
+        return lax.dot_general(x, y, (dims, ((), ())), preferred_element_type=jnp.float32)
+
+    return one(a[0], b[1]) + one(a[1], b[0]) + one(a[0], b[0])
+
+
+NN = ((1,), (0,))
+TN = ((0,), (0,))
+
+
+def root_kernel(flag_ref, a_ref, b_ref, z_ref, work, inv_ref, hi_ref, lo_ref):
+    count = SB // 128
+    chunk = 512
+    work[:, :SB] = a_ref[...]
+    work[:, SB:] = b_ref[...]
+
+    def rows_of(i):
+        return pl.ds(pl.multiple_of(i * 128, 128), 128)
+
+    def cols_of(c):
+        return pl.ds(pl.multiple_of(c * chunk, chunk), chunk)
+
+    def step(i, _):
+        here = rows_of(i)
+        u, w = factor128(work[here, here])
+        inv_ref[i] = w
+        w2 = split(w)
+
+        def scale(c, _):
+            new = dot3(w2, split(work[here, cols_of(c)]), NN)
+            hi, lo = split(new)
+            work[here, cols_of(c)] = new
+            hi_ref[:, cols_of(c)] = hi
+            lo_ref[:, cols_of(c)] = lo
+            return 0
+
+        lax.fori_loop(i * 128 // chunk, 2 * SB // chunk, scale, 0)
+
+        def trail(j, _):
+            there = rows_of(j)
+            left = (hi_ref[:, there], lo_ref[:, there])
+
+            def cols(c, _):
+                right = (hi_ref[:, cols_of(c)], lo_ref[:, cols_of(c)])
+                work[there, cols_of(c)] -= dot3(left, right, TN)
+                return 0
+
+            lax.fori_loop(j * 128 // chunk, 2 * SB // chunk, cols, 0)
+            return 0
+
+        lax.fori_loop(i + 1, count, trail, 0)
+        return 0
+
+    lax.fori_loop(0, count, step, 0)
+
+    @pl.when(flag_ref[0] == 1)
+    def _():
+        row = lax.broadcasted_iota(jnp.int32, (SB, SB), 0)
+        col = lax.broadcasted_iota(jnp.int32, (SB, SB), 1)
+        work[:, SB:] = jnp.where(row == col, -1.0, 0.0)
+
+    def back(n, _):
+        i = count - 1 - n
+        here = rows_of(i)
+        w2 = split(inv_ref[i])
+
+        def cols(c, _):
+            right = split(work[here, cols_of(c)])
+            new = dot3(w2, right, TN)
+            z_ref[here, pl.ds(pl.multiple_of(c * chunk - SB, chunk), chunk)] = new
+            hi, lo = split(new)
+
+            def above(j, _):
+                there = rows_of(j)
+                work[there, cols_of(c)] -= dot3(split(work[there, here]), (hi, lo), NN)
+                return 0
+
+            lax.fori_loop(0, i, above, 0)
+            return 0
+
+        lax.fori_loop(SB // chunk, 2 * SB // chunk, cols, 0)
+        return 0
+
+    lax.fori_loop(0, count, back, 0)
+
+
+def root_solve(flag, a, b):
+    return pl.pallas_call(
+        root_kernel,
+        out_shape=jax.ShapeDtypeStruct((SB, SB), jnp.float32),
+        in_specs=[
+            pl.BlockSpec(memory_space=pltpu.SMEM),
+            pl.BlockSpec(memory_space=pltpu.VMEM),
+            pl.BlockSpec(memory_space=pltpu.VMEM),
+        ],
+        out_specs=pl.BlockSpec(memory_space=pltpu.VMEM),
+        scratch_shapes=[
+            pltpu.VMEM((SB, 2 * SB), jnp.float32),
+            pltpu.VMEM((SB // 128, 128, 128), jnp.float32),
+            pltpu.VMEM((128, 2 * SB), jnp.bfloat16),
+            pltpu.VMEM((128, 2 * SB), jnp.bfloat16),
+        ],
+        compiler_params=pltpu.CompilerParams(vmem_limit_bytes=40 * 2**20),
+    )(flag, a, b)
+
+
+def root_phase(deltas, points, row_at, col_at, row_count, col_count):
+    skel_count = deltas.shape[1]
+    row_width = skel_count // row_count
+    col_width = skel_count // col_count
+    box_total = row_count * col_count
+    lead = SB // box_total
+    shape = (row_count, col_count, 9)
+    tile = jnp.transpose(
+        deltas.reshape(9, col_count, col_width, row_count, row_width), (3, 1, 0, 2, 4)
+    ).reshape(shape + (col_width * row_width,))
+    rows_piece = jnp.transpose(
+        deltas[:, :lead].reshape(9, lead, row_count, row_width), (2, 0, 1, 3)
+    ).reshape(row_count, 1, 9, lead * row_width)
+    cols_piece = jnp.transpose(
+        deltas[:, :, :lead].reshape(9, col_count, col_width, lead), (1, 0, 2, 3)
+    ).reshape(1, col_count, 9, col_width * lead)
+    corner_piece = deltas[:, :lead, :lead].reshape(1, 1, 9, lead * lead)
+    pieces = [tile, rows_piece, cols_piece, corner_piece]
+    sizes = [x.shape[3] for x in pieces]
+    outgoing = jnp.concatenate(
+        [jnp.broadcast_to(x, shape + x.shape[3:]) for x in pieces], axis=3
+    ).reshape(box_total, 9, sum(sizes))
+    arrived = lax.all_to_all(outgoing, ("row", "col"), split_axis=0, concat_axis=0, tiled=True)
+    received = jnp.transpose(arrived, (1, 2, 0))
+    all_skeleton = lax.all_gather(points[:, :skel_count][None], ("row", "col"), axis=0, tiled=True)
+    ordered = jnp.transpose(all_skeleton, (1, 2, 0))
+
+    box_ids = jnp.arange(box_total, dtype=jnp.int32)
+    src_rows = (box_ids // col_count)[None, :]
+    src_cols = (box_ids % col_count)[None, :]
+    hits = []
+    for a, b in offsets_all():
+        living = (
+            (src_rows + a >= 0)
+            & (src_rows + a < row_count)
+            & (src_cols + b >= 0)
+            & (src_cols + b < col_count)
+        )
+        hits.append((box_ids[:, None] == (src_rows + a) * col_count + src_cols + b) & living)
+
+    def coords(start, width):
+        part = lax.dynamic_slice_in_dim(ordered, start, width, 1)
+        return part.reshape(2, width * box_total)
+
+    starts = [0]
+    for size in sizes:
+        starts.append(starts[-1] + size)
+
+    def block(which, row_coords, col_coords):
+        rows_n = row_coords.shape[1] // box_total
+        cols_n = col_coords.shape[1] // box_total
+        part = received[:, starts[which] : starts[which + 1]]
+        part = jnp.transpose(part.reshape(9, cols_n, rows_n, box_total), (0, 2, 1, 3))
+        placed = jnp.zeros((rows_n, box_total, cols_n, box_total), jnp.float32)
+        for n in range(9):
+            placed = jnp.where(hits[n][None, :, None, :], part[n][:, None, :, :], placed)
+        return kernel(row_coords, col_coords) + placed.reshape(
+            rows_n * box_total, cols_n * box_total
+        )
+
+    row_coords = coords(row_at * row_width, row_width)
+    col_coords = coords(col_at * col_width, col_width)
+    lead_coords = coords(0, lead)
+    flag = (col_at == 0).astype(jnp.int32)
+    inner = block(3, lead_coords, lead_coords)
+    across = block(2, lead_coords, col_coords)
+    factor = root_solve(flag[None], inner, across)
+    down = block(1, row_coords, lead_coords)
+    own = block(0, row_coords, col_coords)
+    update = jnp.dot(down, factor, precision=lax.Precision.HIGH)
+    result = jnp.where(col_at == 0, 0.0, own) - update
+    rows_here, cols_here = result.shape
+    global_rows = row_at * rows_here + jnp.arange(rows_here, dtype=jnp.int32)[:, None]
+    global_cols = col_at * cols_here + jnp.arange(cols_here, dtype=jnp.int32)[None, :]
+    return jnp.where((global_rows < SB) & (global_cols > global_rows), 0.0, result)
+
+
 def on_device(offsets, point_order, nugget, interp):
     row_at = lax.axis_index("row")
     col_at = lax.axis_index("col")
@@ -178,95 +409,17 @@
             stored,
         )
         stored = stored + spread(factor_new, move_first, move_second, leading)
-    row_width = skel_count // row_count
-    col_width = skel_count // col_count
-    box_total = row_count * col_count
     weights_skel = weights[:skel_count]
-    row_ids = jnp.arange(skel_count, dtype=jnp.int32).reshape(row_count, row_width)
-    col_ids = jnp.arange(skel_count, dtype=jnp.int32).reshape(col_count, col_width)
-    diag_piece = jnp.where(
-        row_ids[:, None, :, None] == col_ids[None, :, None, :],
-        weights_skel.reshape(row_count, row_width)[:, None, :, None],
-        0.0,
-    )
     pieces = []
     for k, m in enumerate(offsets_all()):
         left_rows, right_rows = cross_pair(stored, m, skel_count)
-        fill_part = jnp.einsum(
-            "rak,rbl->abkl",
-            left_rows.reshape(-1, row_count, row_width),
-            right_rows.reshape(-1, col_count, col_width),
-            precision=highest,
-        )
+        fill_part = jnp.einsum("rk,rl->kl", left_rows, right_rows, precision=highest)
         if m == (0, 0):
-            delta_block = diag_piece - fill_part
+            delta_block = jnp.diag(weights_skel) - fill_part
         else:
             delta_block = -fill_part
         pieces.append(delta_block * present[k])
-    outgoing = jnp.stack(pieces, axis=2).reshape(box_total * 9, row_width * col_width)
-    arrived = lax.all_to_all(outgoing, ("row", "col"), split_axis=0, concat_axis=0, tiled=True)
-    received = jnp.transpose(arrived.reshape(box_total, 9, row_width, col_width), (1, 2, 0, 3))
-    box_ids = jnp.arange(box_total, dtype=jnp.int32)
-    src_rows = (box_ids // col_count)[:, None]
-    src_cols = (box_ids % col_count)[:, None]
-    all_skeleton = lax.all_gather(points[:, :skel_count][None], ("row", "col"), axis=0, tiled=True)
-    row_part = lax.dynamic_slice_in_dim(all_skeleton, row_at * row_width, row_width, 2)
-    col_part = lax.dynamic_slice_in_dim(all_skeleton, col_at * col_width, col_width, 2)
-    row_coords = jnp.transpose(row_part, (1, 2, 0)).reshape(2, row_width * box_total)
-    col_coords = jnp.transpose(col_part, (1, 2, 0)).reshape(2, col_width * box_total)
-    placed = jnp.zeros((row_width, box_total, col_width, box_total), jnp.float32)
-    for n, (a, b) in enumerate(offsets_all()):
-        target = (src_rows + a) * col_count + src_cols + b
-        living = (
-            (src_rows + a >= 0)
-            & (src_rows + a < row_count)
-            & (src_cols + b >= 0)
-            & (src_cols + b < col_count)
-        )
-        hit = (target == box_ids[None, :]) & living
-        placed = jnp.where(hit[None, :, None, :], received[n][:, :, :, None], placed)
-    delta_tile = placed.reshape(row_width * box_total, col_width * box_total)
-    root_matrix = kernel(row_coords, col_coords) + delta_tile
-    rows_here = root_matrix.shape[0]
-    cols_here = root_matrix.shape[1]
-    global_rows = row_at * rows_here + jnp.arange(rows_here, dtype=jnp.int32)
-    global_cols = col_at * cols_here + jnp.arange(cols_here, dtype=jnp.int32)
-    columns_out = []
-    for p in range(2):
-        first_col = p * PW
-        owner_col = first_col // cols_here
-        local_col = first_col % cols_here
-        owner_row = first_col // rows_here
-        local_row = first_col % rows_here
-        own_slab = root_matrix[:, local_col : local_col + PW]
-        slab_rows = spread_2(own_slab, "col", owner_col)
-        diag_block = spread_2(slab_rows[local_row : local_row + PW], "row", owner_row)
-        diag_factor = jnp.linalg.cholesky(diag_block)
-        solved = jax.scipy.linalg.solve_triangular(diag_factor, slab_rows.T, lower=True).T
-        pasted = lax.dynamic_update_slice(solved, diag_factor, (first_col - row_at * rows_here, 0))
-        inside = (global_rows >= first_col) & (global_rows < first_col + PW)
-        panel_rows = jnp.where(
-            (global_rows < first_col)[:, None], 0.0, jnp.where(inside[:, None], pasted, solved)
-        )
-        first_global = col_at * cols_here
-        holder = first_global // rows_here
-        offset_rows = first_global - holder * rows_here
-        panel_cols = spread_2(
-            lax.dynamic_slice_in_dim(panel_rows, offset_rows, cols_here, 0), "row", holder
-        )
-        root_matrix = root_matrix - jnp.einsum(
-            "rk,ck->rc", panel_rows, panel_cols, precision=highest
-        )
-        columns_out.append((owner_col, local_col, panel_rows))
-    for owner_col, local_col, panel_rows in columns_out:
-        current = root_matrix[:, local_col : local_col + PW]
-        root_matrix = lax.dynamic_update_slice(
-            root_matrix, jnp.where(col_at == owner_col, panel_rows, current), (0, local_col)
-        )
-    top_rows = min(2 * PW, rows_here)
-    top_block = root_matrix[:top_rows]
-    zero_mask = (global_rows[:top_rows, None] < 2 * PW) & (global_cols[None, :] >= 2 * PW)
-    return lax.dynamic_update_slice(root_matrix, jnp.where(zero_mask, 0.0, top_block), (0, 0))
+    return root_phase(jnp.stack(pieces), points, row_at, col_at, row_count, col_count)
 
 
 def solution(mesh):

time: 1660 us -> 980 us (0.59)
  waiting for transfers between devices: 610 us -> 206 us
  other arithmetic: 345 us -> 78.6 us
  Pallas kernels: 0 us -> 89.6 us
  local copies, waits for them, and re-layouts: 267 us -> 220 us
  matrix products: 92.8 us -> 49.4 us
  between operations: 22 us -> 3.35 us
    psum x6 -> x0, waiting for transfers between devices: 456 us -> none  [spread_2(): return lax.psum(kept, axis)]
    another operation x39 -> x0, other arithmetic: 241 us -> none  [the longest x30 159 us: on_device(): diag_factor = jnp.linalg.cholesky(diag_block)]
    pallas_call x0 -> x1, Pallas kernels: none -> 89.6 us  [root_solve(): pl.pallas_call(root_kernel, out_shape=jax.ShapeDtypeStruct((SB, SB), jnp....]
    ppermute x16, waiting for transfers between devices: 129 us -> 161 us  [shifted(): return lax.ppermute(block, axis, route)]
    another operation x26 -> x0, matrix products: 27 us -> none  [the longest x14 22.3 us: on_device(): jax.scipy.linalg.solve_triangular(diag_factor, slab_rows.T, lower=True)]
    unnamed x365 -> x329, local copies, waits for them, and re-layouts: 152 us -> 128 us
    all_to_all x1, waiting for transfers between devices: 18.5 us -> 38.8 us  [root_phase(): lax.all_to_all(outgoing, ('row', 'col'), split_axis=0, concat_axis=0, til...]
    another operation x80 -> x10, local copies, waits for them, and re-layouts: 24 us -> 5.76 us  [on_device(): jnp.stack(pieces)]
  transfers between devices with their start and end apart: 27 -> 21, of which waited for: 23 -> 18; matrix products, arithmetic and copies ran while one was open for 3% -> 5% of each run, Pallas kernels for 0% -> 0%
where the time goes in v1:
time: 980 us; the launch traced here: 973 us
  local copies, waits for them, and re-layouts  220 us (22%)
  starting transfers between devices  215 us (22%)
  waiting for transfers between devices  206 us (21%)
  Pallas kernels  89.6 us (9%)
  blocking collectives  87.1 us (9%)
  other arithmetic  78.6 us (8%)
  matrix products  49.4 us (5%)
  loops' own time  23.8 us (2%)
    ppermute x16, starting transfers between devices, shifted(): return lax.ppermute(block, axis, route)  195 us
    ppermute x16, waiting for transfers between devices, shifted(): return lax.ppermute(block, axis, route)  161 us
    unnamed x329, local copies, waits for them, and re-layouts  128 us
    pallas_call x1, Pallas kernels, root_solve(): pl.pallas_call(root_kernel, out_shape=jax.ShapeDtypeStruct((SB, SB), jnp....  89.6 us
    all_gather x1, blocking collectives, root_phase(): lax.all_gather(points[:, :skel_count][None], ('row', 'col'), axis=0, tile...  87.1 us
    all_to_all x1, waiting for transfers between devices, root_phase(): lax.all_to_all(outgoing, ('row', 'col'), split_axis=0, concat_axis=0, til...  38.8 us
    dot_general x1, matrix products, root_phase(): update = jnp.dot(down, factor, precision=lax.Precision.HIGH)  24.8 us
    another operation x4, loops' own time, on_device(): lax.cond(colour == k, lambda s: eliminate(s, near_matrix, interp_box), la...  23.8 us
  transfers between devices with their start and end apart: 21, of which 18 were waited for; matrix products, arithmetic and copies ran while one was open for 5% of the time, Pallas kernels for 0%

profile of v1, /device:TPU:1, one launch (start us, length us, event | category | flops | bytes accessed | tf_op | source)
XLA Modules:
  0.0 972.6 jit_solution(6712469122959208623)
XLA Ops:
  5.1 4.9 collective-permute-start
  25.6 21.3 %conditional.4 = (f32[128,256]{1,0:T(8,128)}, f32[128,256]{1,0:T(8,128)}, f32[128,256]{1,0:T(8,128)}, f32[128,256]{1,0:T(8,128)}, f32[128,256]{1,0:T(8,128)}, /*...) conditional(s32[]{:T(128)} %convert_element_type.48, () %tuple.63, ...), branch_computations={%region_0.1_spmd, %region_1.6_spmd} | conditional | flops 2442133504 | bytes 22315710 | solution.py:405
  65.7 37.3 %collective-permute-start.4 = (f32[6,128,256]{2,1,0:T(8,128)S(1)}, f32[6,128,256]{2,1,0:T(8,128)S(1)}, u32[]{:S(2)}, u32[]{:S(2)}) collective-permute-start(f32[6,128,256]{2,1,0:T(8,128)S(1)} %get-tuple-element.953), channel_id=1, source_target_pairs={{0,16},{16,32},{32,48},{48,64},{64,80},{80,96},{96,112},{1,17},{17... | collective-permute-start | bytes 2359304 | tf_op jit(solution)/shard_map/ppermute | solution.py:33
  106.8 5.1 collective-permute-done.4
  123.8 28.6 %collective-permute-done.6 = f32[14,128,256]{2,1,0:T(8,128)} collective-permute-done((f32[14,128,256]{2,1,0:T(8,128)}, f32[14,128,256]{2,1,0:T(8,128)}, u32[]{:S(2)}, u32[]{:S(2)}) %collective-permute-start.6) | collective-permute-done | bytes 1835040 | tf_op jit(solution)/shard_map/ppermute | solution.py:33
  171.7 8.0 conditional.5
  188.8 10.3 %collective-permute-start.8 = (f32[6,128,256]{2,1,0:T(8,128)S(1)}, f32[6,128,256]{2,1,0:T(8,128)S(1)}, u32[]{:S(2)}, u32[]{:S(2)}) collective-permute-start(f32[6,128,256]{2,1,0:T(8,128)S(1)} %get-tuple-element.941), channel_id=1, source_target_pairs={{0,16},{16,32},{32,48},{48,64},{64,80},{80,96},{96,112},{1,17},{17... | collective-permute-start | bytes 2359304 | tf_op jit(solution)/shard_map/ppermute | solution.py:33
  208.2 5.2 collective-permute-done.9
  213.5 57.2 %collective-permute-start.10 = (f32[14,128,256]{2,1,0:T(8,128)S(1)}, f32[14,128,256]{2,1,0:T(8,128)S(1)}, u32[]{:S(2)}, u32[]{:S(2)}) collective-permute-start(f32[14,128,256]{2,1,0:T(8,128)S(1)} %get-tuple-element.816), channel_id=1, source_target_pairs={{0,1},{1,2},{2,3},{3,4},{4,5},{5,6},{6,7},{7,8},{8,9},{9,10},{10,1... | collective-permute-start | bytes 5505032 | tf_op jit(solution)/shard_map/ppermute | solution.py:33
  277.8 23.6 %collective-permute-done.10 = f32[14,128,256]{2,1,0:T(8,128)S(1)} collective-permute-done((f32[14,128,256]{2,1,0:T(8,128)S(1)}, f32[14,128,256]{2,1,0:T(8,128)S(1)}, u32[]{:S(2)}, u32[]{:S(2)}) %collective-permute-start.10) | collective-permute-done | bytes 1835040 | tf_op jit(solution)/shard_map/ppermute | solution.py:33
  301.6 5.0 collective-permute-done.11
  317.2 69.1 %conditional.6 = (f32[1,128,256]{2,1,0:T(8,128)}, f32[1,128,256]{2,1,0:T(8,128)}, f32[1,128,256]{2,1,0:T(8,128)}, f32[1,128,256]{2,1,0:T(8,128)}, f32[1,128,256]...) conditional(s32[]{:T(128)} %convert_element_type.50, () %tuple.67, ...), branch_computations={%region_6.9_spmd, %region_7.10_spmd} | conditional | flops 5867831296 | bytes 52954240 | solution.py:405
  355.1 13.2 %cholesky.96 = f32[128,128]{1,0:T(8,128)} custom-call(f32[128,128]{1,0:T(8,128)} %fusion.139), custom_call_target="Cholesky" | custom-call | tf_op jit(solution)/shard_map/cond/branch_1_fun/jit(cholesky)/cholesky | solution.py:91
  371.9 11.3 %custom-call.10 = f32[1,128,128]{1,2,0:T(8,128)} custom-call(f32[1,128,128]{2,1,0:T(8,128)} %fusion.135), custom_call_target="InvertDiagBlocksLowerTriangular" | custom-call | tf_op jit(solution)/shard_map/cond/branch_1_fun/jit(_solve_triangular)/triangular_solve | solution.py:92
  418.0 13.6 %collective-permute-done.13 = f32[6,128,256]{2,1,0:T(8,128)S(1)} collective-permute-done((f32[6,128,256]{2,1,0:T(8,128)S(1)}, f32[6,128,256]{2,1,0:T(8,128)S(1)}, u32[]{:S(2)}, u32[]{:S(2)}) %collective-permute-start.13) | collective-permute-done | bytes 786464 | tf_op jit(solution)/shard_map/ppermute | solution.py:33
  438.3 19.9 %collective-permute-done.14 = f32[14,128,256]{2,1,0:T(8,128)} collective-permute-done((f32[14,128,256]{2,1,0:T(8,128)}, f32[14,128,256]{2,1,0:T(8,128)}, u32[]{:S(2)}, u32[]{:S(2)}) %collective-permute-start.14) | collective-permute-done | bytes 1835040 | tf_op jit(solution)/shard_map/ppermute | solution.py:33
  460.5 5.4 collective-permute-done.15
  485.9 6.6 add.796
  492.5 10.6 %conditional.7 = (f32[1,128,256]{2,1,0:T(8,128)S(1)}, f32[1,128,256]{2,1,0:T(8,128)S(1)}, f32[1,128,256]{2,1,0:T(8,128)S(1)}, f32[1,128,256]{2,1,0:T(8,128)S(1)}...) conditional(s32[]{:T(128)} %convert_element_type.51, () %tuple.69, ...), branch_computations={%region_8.11_spmd, %region_9.12_spmd} | conditional | flops 5867831296 | bytes 52429896 | solution.py:405
  514.5 17.7 %collective-permute-start.16 = (f32[6,128,256]{2,1,0:T(8,128)S(1)}, f32[6,128,256]{2,1,0:T(8,128)S(1)}, u32[]{:S(2)}, u32[]{:S(2)}) collective-permute-start(f32[6,128,256]{2,1,0:T(8,128)S(1)} %get-tuple-element.917), channel_id=1, source_target_pairs={{0,16},{16,32},{32,48},{48,64},{64,80},{80,96},{96,112},{1,17},{17... | collective-permute-start | bytes 2359304 | tf_op jit(solution)/shard_map/ppermute | solution.py:33
  536.5 4.7 collective-permute-done.16
  547.7 52.5 %collective-permute-start.18 = (f32[14,128,256]{2,1,0:T(8,128)}, f32[14,128,256]{2,1,0:T(8,128)}, u32[]{:S(2)}, u32[]{:S(2)}) collective-permute-start(f32[14,128,256]{2,1,0:T(8,128)} %get-tuple-element.800), channel_id=1, source_target_pairs={{0,1},{1,2},{2,3},{3,4},{4,5},{5,6},{6,7},{7,8},{8,9},{9,10},{10,1... | collective-permute-start | bytes 5505032 | tf_op jit(solution)/shard_map/ppermute | solution.py:33
  600.2 87.1 %all-gather.1 = f32[128,2,128]{2,1,0:T(2,128)} all-gather(f32[1,2,128]{2,1,0:T(2,128)S(1)} %copy.91), channel_id=2, replica_groups=mesh['row'=8,'col'=16] {'row','col'}, dimensions={0}, use_global_device_ids=true | all-gather | bytes 132096 | tf_op jit(solution)/shard_map/all_gather | solution.py:313
  701.9 32.0 %collective-permute-done.19 = f32[14,128,256]{2,1,0:T(8,128)S(1)} collective-permute-done((f32[14,128,256]{2,1,0:T(8,128)S(1)}, f32[14,128,256]{2,1,0:T(8,128)S(1)}, u32[]{:S(2)}, u32[]{:S(2)}) %collective-permute-start.19) | collective-permute-done | bytes 1835040 | tf_op jit(solution)/shard_map/ppermute | solution.py:33
  764.8 14.3 %concatenate.333 = f32[128,9,128]{2,0,1:T(8,128)S(1)} reshape(f32[8,16,9,8,16]{4,3,1,0,2:T(8,128)} %bitcast.926) | data formatting | bytes 1179648 | tf_op jit(solution)/shard_map/concatenate | solution.py:308
  783.2 7.8 all-to-all-start
  793.3 38.8 %all-to-all-done = f32[128,9,384]{2,1,0:T(8,128)S(1)} async-done(((f32[128,9,384]{2,1,0:T(8,128)}), f32[128,9,384]{2,1,0:T(8,128)S(1)}, u32[]{:S(2)}, u32[]{:S(2)}) %all-to-all-start) | async-done | bytes 1769504 | tf_op jit(solution)/shard_map/all_to_all | solution.py:311
  841.7 5.0 bitcast_add_fusion.7
  846.7 89.6 %shard_map.46 = f32[1024,1024]{1,0:T(8,128)S(1)} custom-call(s32[1]{0:T(128)} %bitcast.312.flag_ref, f32[1024,1024]{1,0:T(8,128)S(1)} %get-tuple-element.960.a_ref, f32[1024,1024]{1,0:T(8,128)S(1)} %get-tuple-element.959.b_ref), custom_call_target="tpu_custom_call" | custom-call | tf_op jit(solution)/shard_map/pallas_call | solution.py:270
  936.3 5.4 select_select_fusion.4
  941.8 5.4 select_select_fusion.5
  947.3 24.8 %fusion.215 = f32[2048,1024]{1,0:T(8,128)} fusion(f32[256,8,8,128]{3,2,1,0:T(8,128)S(1)} %bitcast.923, f32[1024,1024]{1,0:T(8,128)S(1)} %shard_map.46, f32[256,8,8,128]{3,2,1,0:T(8,128)S(1)} %bitcast.922, f32[1024]{0:T(1024)S(1)} %copy-done.46, f32[1024]{0:T(1024)S(1)} %copy-done.45, f32[1024]{0:T(1024)S(1)} %copy-done.48, f32[2048]{0:T(1024)S(1)} %copy-done.52, ...), kind=kOutput, calls=%fused_computation.552 | convolution fusion | flops 12933136384 | bytes 29407232 | tf_op jit(solution)/shard_map/dot_general | solution.py:358
  (606 shorter events, 312.9 us)
Async XLA Ops:
  5.1 7.4 collective-permute-start
  10.0 6.3 collective-permute-start.1
  16.4 4.9 collective-permute-start.2
  19.6 4.4 collective-permute-start.3
  54.2 49.7 %copy-start.20 = (f32[1,128,256]{2,1,0:T(8,128)S(1)}, f32[1,128,256]{2,1,0:T(8,128)}, u32[]{:S(2)}) copy-start(f32[1,128,256]{2,1,0:T(8,128)} %copy-done.19) | copy-start | bytes 393220
  65.7 46.2 %collective-permute-start.4 = (f32[6,128,256]{2,1,0:T(8,128)S(1)}, f32[6,128,256]{2,1,0:T(8,128)S(1)}, u32[]{:S(2)}, u32[]{:S(2)}) collective-permute-start(f32[6,128,256]{2,1,0:T(8,128)S(1)} %get-tuple-element.953), channel_id=1, source_target_pairs={{0,16},{16,32},{32,48},{48,64},{64,80},{80,96},{96,112},{1,17},{17... | collective-permute-start | bytes 2359304 | tf_op jit(solution)/shard_map/ppermute | solution.py:33
  104.9 13.3 %collective-permute-start.5 = (f32[6,128,256]{2,1,0:T(8,128)S(1)}, f32[6,128,256]{2,1,0:T(8,128)S(1)}, u32[]{:S(2)}, u32[]{:S(2)}) collective-permute-start(f32[6,128,256]{2,1,0:T(8,128)S(1)} %constant_dynamic-update-slice_fusion.190), channel_id=1, source_target_pairs={{16,0},{32,16},{48,32},{64,48},{80,64},{96,80},{112,96},{17,1},{33... | collective-permute-start | bytes 2359304 | tf_op jit(solution)/shard_map/ppermute | solution.py:33
  119.9 32.5 %collective-permute-start.6 = (f32[14,128,256]{2,1,0:T(8,128)}, f32[14,128,256]{2,1,0:T(8,128)}, u32[]{:S(2)}, u32[]{:S(2)}) collective-permute-start(f32[14,128,256]{2,1,0:T(8,128)} %get-tuple-element.824), channel_id=1, source_target_pairs={{0,1},{1,2},{2,3},{3,4},{4,5},{5,6},{6,7},{7,8},{8,9},{9,10},{10,1... | collective-permute-start | bytes 5505032 | tf_op jit(solution)/shard_map/ppermute | solution.py:33
  122.5 35.5 %collective-permute-start.7 = (f32[14,128,256]{2,1,0:T(8,128)}, f32[14,128,256]{2,1,0:T(8,128)}, u32[]{:S(2)}, u32[]{:S(2)}) collective-permute-start(f32[14,128,256]{2,1,0:T(8,128)} %get-tuple-element.823), channel_id=1, source_target_pairs={{1,0},{2,1},{3,2},{4,3},{5,4},{6,5},{7,6},{8,7},{9,8},{10,9},{11,1... | collective-permute-start | bytes 5505032 | tf_op jit(solution)/shard_map/ppermute | solution.py:33
  188.8 19.2 %collective-permute-start.8 = (f32[6,128,256]{2,1,0:T(8,128)S(1)}, f32[6,128,256]{2,1,0:T(8,128)S(1)}, u32[]{:S(2)}, u32[]{:S(2)}) collective-permute-start(f32[6,128,256]{2,1,0:T(8,128)S(1)} %get-tuple-element.941), channel_id=1, source_target_pairs={{0,16},{16,32},{32,48},{48,64},{64,80},{80,96},{96,112},{1,17},{17... | collective-permute-start | bytes 2359304 | tf_op jit(solution)/shard_map/ppermute | solution.py:33
  200.1 13.3 %collective-permute-start.9 = (f32[6,128,256]{2,1,0:T(8,128)S(1)}, f32[6,128,256]{2,1,0:T(8,128)S(1)}, u32[]{:S(2)}, u32[]{:S(2)}) collective-permute-start(f32[6,128,256]{2,1,0:T(8,128)S(1)} %constant_dynamic-update-slice_fusion.246), channel_id=1, source_target_pairs={{16,0},{32,16},{48,32},{64,48},{80,64},{96,80},{112,96},{17,1},{33... | collective-permute-start | bytes 2359304 | tf_op jit(solution)/shard_map/ppermute | solution.py:33
  213.5 88.0 %collective-permute-start.10 = (f32[14,128,256]{2,1,0:T(8,128)S(1)}, f32[14,128,256]{2,1,0:T(8,128)S(1)}, u32[]{:S(2)}, u32[]{:S(2)}) collective-permute-start(f32[14,128,256]{2,1,0:T(8,128)S(1)} %get-tuple-element.816), channel_id=1, source_target_pairs={{0,1},{1,2},{2,3},{3,4},{4,5},{5,6},{6,7},{7,8},{8,9},{9,10},{10,1... | collective-permute-start | bytes 5505032 | tf_op jit(solution)/shard_map/ppermute | solution.py:33
  271.6 35.0 %collective-permute-start.11 = (f32[14,128,256]{2,1,0:T(8,128)S(1)}, f32[14,128,256]{2,1,0:T(8,128)S(1)}, u32[]{:S(2)}, u32[]{:S(2)}) collective-permute-start(f32[14,128,256]{2,1,0:T(8,128)S(1)} %get-tuple-element.815), channel_id=1, source_target_pairs={{1,0},{2,1},{3,2},{4,3},{5,4},{6,5},{7,6},{8,7},{9,8},{10,9},{11,1... | collective-permute-start | bytes 5505032 | tf_op jit(solution)/shard_map/ppermute | solution.py:33
  405.5 10.8 %collective-permute-start.12 = (f32[6,128,256]{2,1,0:T(8,128)S(1)}, f32[6,128,256]{2,1,0:T(8,128)S(1)}, u32[]{:S(2)}, u32[]{:S(2)}) collective-permute-start(f32[6,128,256]{2,1,0:T(8,128)S(1)} %get-tuple-element.929), channel_id=1, source_target_pairs={{0,16},{16,32},{32,48},{48,64},{64,80},{80,96},{96,112},{1,17},{17... | collective-permute-start | bytes 2359304 | tf_op jit(solution)/shard_map/ppermute | solution.py:33
  408.3 29.4 %copy-start.31 = (f32[2,256]{0,1:T(8,128)S(1)}, f32[2,256]{0,1:T(8,128)}, u32[]{:S(2)}) copy-start(f32[2,256]{0,1:T(8,128)} %copy-done.30) | copy-start | bytes 6148
  410.2 21.4 %collective-permute-start.13 = (f32[6,128,256]{2,1,0:T(8,128)S(1)}, f32[6,128,256]{2,1,0:T(8,128)S(1)}, u32[]{:S(2)}, u32[]{:S(2)}) collective-permute-start(f32[6,128,256]{2,1,0:T(8,128)S(1)} %constant_dynamic-update-slice_fusion.302), channel_id=1, source_target_pairs={{16,0},{32,16},{48,32},{64,48},{80,64},{96,80},{112,96},{17,1},{33... | collective-permute-start | bytes 2359304 | tf_op jit(solution)/shard_map/ppermute | solution.py:33
  433.3 24.9 %collective-permute-start.14 = (f32[14,128,256]{2,1,0:T(8,128)}, f32[14,128,256]{2,1,0:T(8,128)}, u32[]{:S(2)}, u32[]{:S(2)}) collective-permute-start(f32[14,128,256]{2,1,0:T(8,128)} %get-tuple-element.808), channel_id=1, source_target_pairs={{0,1},{1,2},{2,3},{3,4},{4,5},{5,6},{6,7},{7,8},{8,9},{9,10},{10,1... | collective-permute-start | bytes 5505032 | tf_op jit(solution)/shard_map/ppermute | solution.py:33
  435.9 30.1 %collective-permute-start.15 = (f32[14,128,256]{2,1,0:T(8,128)}, f32[14,128,256]{2,1,0:T(8,128)}, u32[]{:S(2)}, u32[]{:S(2)}) collective-permute-start(f32[14,128,256]{2,1,0:T(8,128)} %get-tuple-element.807), channel_id=1, source_target_pairs={{1,0},{2,1},{3,2},{4,3},{5,4},{6,5},{7,6},{8,7},{9,8},{10,9},{11,1... | collective-permute-start | bytes 5505032 | tf_op jit(solution)/shard_map/ppermute | solution.py:33
  510.7 22.1 %copy-start.22 = (f32[1,128,256]{2,1,0:T(8,128)S(1)}, f32[1,128,256]{2,1,0:T(8,128)}, u32[]{:S(2)}) copy-start(f32[1,128,256]{2,1,0:T(8,128)} %copy-done.21) | copy-start | bytes 393220
  514.5 26.7 %collective-permute-start.16 = (f32[6,128,256]{2,1,0:T(8,128)S(1)}, f32[6,128,256]{2,1,0:T(8,128)S(1)}, u32[]{:S(2)}, u32[]{:S(2)}) collective-permute-start(f32[6,128,256]{2,1,0:T(8,128)S(1)} %get-tuple-element.917), channel_id=1, source_target_pairs={{0,16},{16,32},{32,48},{48,64},{64,80},{80,96},{96,112},{1,17},{17... | collective-permute-start | bytes 2359304 | tf_op jit(solution)/shard_map/ppermute | solution.py:33
  532.9 13.3 %collective-permute-start.17 = (f32[6,128,256]{2,1,0:T(8,128)S(1)}, f32[6,128,256]{2,1,0:T(8,128)S(1)}, u32[]{:S(2)}, u32[]{:S(2)}) collective-permute-start(f32[6,128,256]{2,1,0:T(8,128)S(1)} %constant_dynamic-update-slice_fusion.358), channel_id=1, source_target_pairs={{16,0},{32,16},{48,32},{64,48},{80,64},{96,80},{112,96},{17,1},{33... | collective-permute-start | bytes 2359304 | tf_op jit(solution)/shard_map/ppermute | solution.py:33
  547.7 153.0 %collective-permute-start.18 = (f32[14,128,256]{2,1,0:T(8,128)}, f32[14,128,256]{2,1,0:T(8,128)}, u32[]{:S(2)}, u32[]{:S(2)}) collective-permute-start(f32[14,128,256]{2,1,0:T(8,128)} %get-tuple-element.800), channel_id=1, source_target_pairs={{0,1},{1,2},{2,3},{3,4},{4,5},{5,6},{6,7},{7,8},{8,9},{9,10},{10,1... | collective-permute-start | bytes 5505032 | tf_op jit(solution)/shard_map/ppermute | solution.py:33
  690.7 43.2 %collective-permute-start.19 = (f32[14,128,256]{2,1,0:T(8,128)S(1)}, f32[14,128,256]{2,1,0:T(8,128)S(1)}, u32[]{:S(2)}, u32[]{:S(2)}) collective-permute-start(f32[14,128,256]{2,1,0:T(8,128)S(1)} %get-tuple-element.799), channel_id=1, source_target_pairs={{1,0},{2,1},{3,2},{4,3},{5,4},{6,5},{7,6},{8,7},{9,8},{10,9},{11,1... | collective-permute-start | bytes 5505032 | tf_op jit(solution)/shard_map/ppermute | solution.py:33
  701.8 33.3 %copy-start.29 = (f32[1,128,256]{2,1,0:T(8,128)S(1)}, f32[1,128,256]{2,1,0:T(8,128)}, u32[]{:S(2)}) copy-start(f32[1,128,256]{2,1,0:T(8,128)} %copy-done.27) | copy-start | bytes 393220
  701.8 33.4 %copy-start.23 = (f32[1,128,256]{2,1,0:T(8,128)S(1)}, f32[1,128,256]{2,1,0:T(8,128)}, u32[]{:S(2)}) copy-start(f32[1,128,256]{2,1,0:T(8,128)} %copy-done.21) | copy-start | bytes 393220
  701.8 33.4 %copy-start.26 = (f32[1,128,256]{2,1,0:T(8,128)S(1)}, f32[1,128,256]{2,1,0:T(8,128)}, u32[]{:S(2)}) copy-start(f32[1,128,256]{2,1,0:T(8,128)} %copy-done.24) | copy-start | bytes 393220
  701.8 33.4 %copy-start.40 = (f32[1,128,256]{2,1,0:T(8,128)S(1)}, f32[1,128,256]{2,1,0:T(8,128)}, u32[]{:S(2)}) copy-start(f32[1,128,256]{2,1,0:T(8,128)} %copy-done.38) | copy-start | bytes 393220
  701.8 33.4 %copy-start.34 = (f32[1,128,256]{2,1,0:T(8,128)S(1)}, f32[1,128,256]{2,1,0:T(8,128)}, u32[]{:S(2)}) copy-start(f32[1,128,256]{2,1,0:T(8,128)} %copy-done.32) | copy-start | bytes 393220
  701.9 34.3 %copy-start.15 = (f32[1,128,256]{2,1,0:T(8,128)S(1)}, f32[1,128,256]{2,1,0:T(8,128)}, u32[]{:S(2)}) copy-start(f32[1,128,256]{2,1,0:T(8,128)} %copy-done.13) | copy-start | bytes 393220
  701.9 34.3 %copy-start.37 = (f32[1,128,256]{2,1,0:T(8,128)S(1)}, f32[1,128,256]{2,1,0:T(8,128)}, u32[]{:S(2)}) copy-start(f32[1,128,256]{2,1,0:T(8,128)} %copy-done.35) | copy-start | bytes 393220
  783.2 48.8 %all-to-all-start = ((f32[128,9,384]{2,1,0:T(8,128)}), f32[128,9,384]{2,1,0:T(8,128)S(1)}, u32[]{:S(2)}, u32[]{:S(2)}) async-start(f32[128,9,384]{2,1,0:T(8,128)} %copy.109), calls=%async_computation | async-start | bytes 6291456 | tf_op jit(solution)/shard_map/all_to_all | solution.py:311
  947.3 24.8 %copy-start.1 = (f32[1,1,256]{2,1,0:T(1,128)S(1)}, f32[1,1,256]{2,1,0:T(1,128)}, u32[]{:S(2)}) copy-start(f32[1,1,256]{2,1,0:T(1,128)} %param.17) | copy-start | bytes 3076
  (55 other events, 277.6 us)
